TPU v7x, 32 devices: a whole 2x2x4 slice. The times are simulated.
32 devices in a mesh: chain: 4 (over z), ctx: 4 (over y, x), tp: 2 (over core).
Axes of the slice: x: 2, y: 2, z: 4, core: 2. Of those that a mesh axis runs over, the one named last changes fastest.
Arguments:
- tokens: bfloat16 [16384, 2048], P(('chain', 'ctx')), may hold values from -6 to 6
- w_in: bfloat16 [2048, 3, 2, 1024], P(None, None, 'tp'), may hold values from -0.125 to 0.125
- conv_w: float32 [3, 3, 2, 1024], P(None, None, 'tp'), may hold values from -3 to 3
- w_q: bfloat16 [2048, 256], replicated, may hold values from -0.125 to 0.125
- w_k: bfloat16 [2048, 256], replicated, may hold values from -0.125 to 0.125
- gain: float32 [2, 1024], P('tp'), may hold values from 0.1 to 1.9
- w_o: bfloat16 [2, 1024, 2048], P('tp'), may hold values from -0.125 to 0.125
Outputs:
- out: bfloat16 [16384, 2048], P(('chain', 'ctx', 'tp'))
All inputs are finite; a program needn't handle non-finite values.
Results may differ from a plain program's by a relative error of at most 0.013.
Values may be sent and summed in bfloat16 or wider, within the bound.
No kernel may reach another device: no remote copies, remote signals or barrier semaphores. Data moves between devices by JAX's collectives and lax.ppermute only.
A program may use at most 192 MiB of HBM per device.

v0:
```python
import math

import jax
import jax.numpy as jnp
from jax import lax
from jax.sharding import PartitionSpec as P

H = 16
F = 16


EPS = 1e-05
HIGH = lax.Precision.HIGHEST


def shifted(block, axis, distance):
    devices = range(lax.axis_size(axis))
    route = [(i - distance, i) for i in devices if i - distance in devices]
    return lax.ppermute(block, axis, route)


def prefix_2(x, axis, combine, identity):
    peers, mine = (lax.axis_size(axis), lax.axis_index(axis))
    everything = jax.tree.map(
        lambda part, kind: lax.all_gather(part.astype(kind), axis),
        x,
        (jnp.bfloat16, jnp.bfloat16, jnp.bfloat16),
    )
    start = jax.tree.map(
        lambda part, zero: jnp.broadcast_to(jnp.asarray(zero, part.dtype), part.shape), x, identity
    )

    def lap(k, before):
        reached = k < mine
        new = combine(
            before, jax.tree.map(lambda part, own: part[k].astype(own.dtype), everything, x)
        )
        return jax.tree.map(lambda a, b: jnp.where(reached, a, b), new, before)

    return lax.fori_loop(0, peers, lap, start)


def second_order(inputs):
    widened = inputs.astype(jnp.float32)
    feature = inputs.shape[-1]
    products = widened[..., :, None] * widened[..., None, :] * (1.0 / math.sqrt(2.0 * feature))
    return products.reshape(inputs.shape[:-1] + (feature * feature,)).astype(jnp.bfloat16)


def combine_states(earlier, later):
    return (earlier[0] + later[0], earlier[1] + later[1], earlier[2] + later[2])


def zero_like_states(totals):
    return (jnp.zeros_like(totals[0]), jnp.zeros_like(totals[1]), jnp.zeros_like(totals[2]))


def block_states(queries, keys, values):
    length, num_heads, feature = queries.shape
    value_dim = values.shape[2]
    block_len = min(512, length)
    block_count = length // block_len
    query_blocks = queries.reshape(block_count, block_len, num_heads, feature)
    key_blocks = keys.reshape(block_count, block_len, num_heads, feature)
    value_blocks = values.reshape(block_count, block_len, num_heads, value_dim)
    qwide_blocks = second_order(query_blocks)
    kwide_blocks = second_order(key_blocks)
    quad_each = jnp.einsum(
        "nbhf,nbhe->nhfe", kwide_blocks, value_blocks, preferred_element_type=jnp.float32
    )
    line_each = jnp.einsum(
        "nbhf,nbhe->nhfe", key_blocks, value_blocks, preferred_element_type=jnp.float32
    )
    flat_each = jnp.sum(value_blocks.astype(jnp.float32), axis=1)
    blocks = (query_blocks, key_blocks, qwide_blocks, kwide_blocks, value_blocks)
    each = (quad_each, line_each, flat_each)
    totals = (jnp.sum(quad_each, axis=0), jnp.sum(line_each, axis=0), jnp.sum(flat_each, axis=0))
    return (blocks, each, totals)


def finish_blocks(blocks, each, prefix):
    query_blocks, key_blocks, qwide_blocks, kwide_blocks, value_blocks = blocks
    block_count, block_len, num_heads, feature = query_blocks.shape
    inv_root = 1.0 / math.sqrt(feature)
    starts = tuple(
        (jnp.cumsum(part, axis=0) - part + whole[None] for part, whole in zip(each, prefix))
    )
    carried = (
        jnp.einsum("nbhf,nhfe->nbhe", qwide_blocks.astype(jnp.float32), starts[0], precision=HIGH)
        + jnp.einsum("nbhf,nhfe->nbhe", query_blocks.astype(jnp.float32), starts[1], precision=HIGH)
        * inv_root
        + starts[2][:, None]
    )
    causal = lax.broadcasted_iota(jnp.int32, (block_len, block_len), 0) >= lax.broadcasted_iota(
        jnp.int32, (block_len, block_len), 1
    )
    kernel = (
        1.0
        + jnp.einsum(
            "nbhf,nchf->nhbc", query_blocks, key_blocks, preferred_element_type=jnp.float32
        )
        * inv_root
        + jnp.einsum(
            "nbhf,nchf->nhbc", qwide_blocks, kwide_blocks, preferred_element_type=jnp.float32
        )
    )
    kernel = jnp.where(causal[None, None], kernel, 0.0).astype(jnp.bfloat16)
    inside = jnp.einsum("nhbc,nche->nbhe", kernel, value_blocks, preferred_element_type=jnp.float32)
    whole = carried + inside
    return whole.reshape(block_count * block_len, num_heads, value_blocks.shape[3])


def group_norm(attended):
    mean_sq = jnp.mean(attended * attended, axis=-1, keepdims=True)
    return (attended * lax.rsqrt(mean_sq + EPS)).astype(jnp.bfloat16)


def per_device(tokens, w_in, conv_w, w_q, w_k, gain, w_o):
    row_count, width = tokens.shape
    half_width = w_in.shape[3]
    head_half = half_width // H
    projected = jnp.dot(
        tokens, w_in.reshape(width, 3 * half_width), preferred_element_type=jnp.float32
    ).astype(jnp.bfloat16)
    projected = projected.reshape(row_count, 3, half_width)
    before = shifted(projected[row_count - 2 :], ("chain", "ctx"), 1)
    extended = jnp.concatenate([before, projected], axis=0)
    filters = conv_w.reshape(3, 3, half_width)
    convolved = (
        filters[0] * extended[2:].astype(jnp.float32)
        + filters[1] * extended[1:-1].astype(jnp.float32)
        + filters[2] * extended[:-2].astype(jnp.float32)
    ).astype(jnp.bfloat16)
    queries = jnp.dot(tokens, w_q, preferred_element_type=jnp.float32).astype(jnp.bfloat16)
    keys = jnp.dot(tokens, w_k, preferred_element_type=jnp.float32).astype(jnp.bfloat16)
    values = convolved[:, 0]
    local_heads = H // lax.axis_size("ctx")
    head_queries, head_keys, head_values = (
        lax.all_to_all(queries, "ctx", split_axis=1, concat_axis=0, tiled=True),
        lax.all_to_all(keys, "ctx", split_axis=1, concat_axis=0, tiled=True),
        lax.all_to_all(values, "ctx", split_axis=1, concat_axis=0, tiled=True),
    )
    group_rows = head_queries.shape[0]
    blocks, each, totals = block_states(
        head_queries.reshape(group_rows, local_heads, F),
        head_keys.reshape(group_rows, local_heads, F),
        head_values.reshape(group_rows, local_heads, head_half),
    )
    prefix = prefix_2(
        (totals[0], totals[1], totals[2]), "chain", combine_states, zero_like_states(totals)
    )
    normed = group_norm(finish_blocks(blocks, each, prefix))
    normed = normed.reshape(group_rows, local_heads * head_half)
    attended = lax.all_to_all(normed, "ctx", split_axis=0, concat_axis=1, tiled=True)
    gains = gain.reshape(half_width)
    mixed = (
        jax.nn.silu(convolved[:, 1].astype(jnp.float32))
        * (attended.astype(jnp.float32) * gains + convolved[:, 2].astype(jnp.float32))
    ).astype(jnp.bfloat16)
    out_weight = w_o.reshape(half_width, width)
    summed = lax.psum_scatter(
        jnp.dot(mixed, out_weight, preferred_element_type=jnp.float32).astype(jnp.bfloat16),
        "tp",
        scatter_dimension=0,
        tiled=True,
    )
    return summed


def solution(mesh):
    return jax.shard_map(
        per_device,
        mesh=mesh,
        in_specs=(
            P(("chain", "ctx"), None),
            P(None, None, "tp", None),
            P(None, None, "tp", None),
            P(),
            P(),
            P("tp", None),
            P("tp", None, None),
        ),
        out_specs=P(("chain", "ctx", "tp"), None),
        check_vma=False,
    )
```

profile of v0, /device:TPU:1, one launch (start us, length us, event | category | flops | bytes accessed | tf_op | source)
XLA Modules:
  0.0 313.4 jit_solution(1322306076198130232)
XLA Ops:
  6.5 17.0 %copy.34 = bf16[2048,3,1,1024]{0,3,1,2:T(8,128)(2,1)} copy(bf16[2048,3,1,1024]{3,0,2,1:T(8,128)(2,1)} %param.10) | data formatting | bytes 25165824 | tf_op args[1]
  23.6 18.1 %convolution_convert_fusion = bf16[1024,3072]{1,0:T(8,128)(2,1)S(1)} fusion(bf16[1024,2048]{1,0:T(8,128)(2,1)} %param.9, bf16[2048,3072]{0,1:T(8,128)(2,1)} %bitcast.91), kind=kOutput, calls=%fused_computation.15 | convolution fusion | flops 12888047616 | bytes 23068672 | tf_op jit(solution)/shard_map/dot_general | solution.py:122
  41.8 4.2 %collective-permute-start = (bf16[2,3,1024]{2,0,1:T(2,128)(2,1)S(1)}, bf16[2,3,1024]{2,0,1:T(2,128)(2,1)S(1)}, u32[]{:S(2)}, u32[]{:S(2)}) collective-permute-start(bf16[2,3,1024]{2,0,1:T(2,128)(2,1)S(1)} %bitcast.99), channel_id=1, source_target_pairs={{0,2},{2,4},{4,6},{6,8},{8,10},{10,12},{12,14},{14,16},{16,18},{18... | collective-permute-start | bytes 36872 | tf_op jit(solution)/shard_map/ppermute | solution.py:19
  46.0 2.1 convolution_convert_fusion.2
  48.1 3.5 %all-to-all-start = ((bf16[1024,4,64]{0,2,1:T(8,128)(2,1)}), bf16[1024,4,64]{0,2,1:T(8,128)(2,1)S(1)}, u32[]{:S(2)}, u32[]{:S(2)}) async-start(bf16[1024,4,64]{0,2,1:T(8,128)(2,1)} %bitcast.3), calls=%async_computation | async-start | bytes 1048576 | tf_op jit(solution)/shard_map/all_to_all | solution.py:140
  51.6 4.3 %convolution_convert_fusion.1 = bf16[1024,256]{0,1:T(8,128)(2,1)} fusion(bf16[1024,2048]{1,0:T(8,128)(2,1)} %param.9, bf16[2048,256]{1,0:T(8,128)(2,1)S(1)} %copy-done.15), kind=kOutput, calls=%fused_computation.41 | convolution fusion | flops 1074003968 | bytes 5767168 | tf_op jit(solution)/shard_map/dot_general | solution.py:134
  56.0 0.8 iota_compare_fusion
  56.8 8.6 %copy.35 = bf16[1024,3072]{0,1:T(8,128)(2,1)} copy(bf16[1024,3072]{1,0:T(8,128)(2,1)} %copy-done.5) | data formatting | bytes 12582912 | tf_op jit(solution)/shard_map/convert_element_type | solution.py:124
  65.9 14.3 %add_convert_fusion = bf16[1024,3,1024]{0,2,1:T(8,128)(2,1)S(1)} fusion(bf16[1024,3,1024]{0,2,1:T(8,128)(2,1)} %bitcast.89, bf16[2,3,1024]{0,2,1:T(8,128)(2,1)S(1)} %copy.37, f32[3,1024]{1,0:T(4,128)S(1)} %get-tuple-element.209, f32[3,1024]{1,0:T(4,128)S(1)} %get-tuple-element.210, f32[3,1024]{1,0:T(4,128)S(1)} %bitcast.98), kind=kLoop, calls=%fused_computation.9 | loop fusion | flops 47185920 | bytes 12632064 | tf_op jit(solution)/shard_map/convert_element_type | solution.py:133
  80.2 2.6 copy-done.2
  82.7 1.5 slice.47
  84.2 3.8 %all-to-all-start.2 = ((bf16[1024,4,64]{0,2,1:T(8,128)(2,1)}), bf16[1024,4,64]{0,2,1:T(8,128)(2,1)S(1)}, u32[]{:S(2)}, u32[]{:S(2)}) async-start(bf16[1024,4,64]{0,2,1:T(8,128)(2,1)} %bitcast.10), calls=%async_computation.2 | async-start | bytes 1048576 | tf_op jit(solution)/shard_map/all_to_all | solution.py:139
  88.8 6.3 %multiply_convert_fusion.1 = bf16[8,512,4,16,16]{1,4,3,2,0:T(8,128)(2,1)} fusion(f32[8,512,4,16]{1,3,2,0:T(8,128)S(1)} %copy.39), kind=kLoop, calls=%fused_computation.6 | loop fusion | flops 12582912 | bytes 9437184 | tf_op jit(solution)/shard_map/convert_element_type | solution.py:47
  95.1 0.8 copy-done.9
  95.9 3.6 %all-to-all-start.1 = ((bf16[1024,4,256]{0,2,1:T(8,128)(2,1)}), bf16[1024,4,256]{0,2,1:T(8,128)(2,1)S(1)}, u32[]{:S(2)}, u32[]{:S(2)}) async-start(bf16[1024,4,256]{0,2,1:T(8,128)(2,1)} %bitcast.92), calls=%async_computation.1 | async-start | bytes 4194304 | tf_op jit(solution)/shard_map/all_to_all | solution.py:141
  99.5 2.3 copy.48
  101.8 2.0 reshape_reshape.11
  103.8 1.2 copy.49
  105.0 6.3 %multiply_convert_fusion = bf16[8,512,4,16,16]{1,4,3,2,0:T(8,128)(2,1)} fusion(f32[8,512,4,16]{1,3,2,0:T(8,128)S(1)} %copy.49), kind=kLoop, calls=%fused_computation.5 | loop fusion | flops 12582912 | bytes 9437184 | tf_op jit(solution)/shard_map/convert_element_type | solution.py:47
  111.3 17.8 %fusion.40 = f32[8,4,512,512]{3,2,1,0:T(8,128)} fusion(bf16[8,512,4,256]{1,3,2,0:T(8,128)(2,1)} %bitcast.83, bf16[8,512,4,256]{1,3,2,0:T(8,128)(2,1)} %bitcast.85), kind=kOutput, calls=%fused_computation.63 | convolution fusion | flops 4294967296 | bytes 50331648 | tf_op jit(solution)/shard_map/nbhf,nchf->nhbc/dot_general | solution.py:103
  129.0 2.9 copy.41
  132.0 4.0 %reshape_reshape.10 = bf16[8,512,4,64]{1,0,3,2:T(8,128)(2,1)} reshape(bf16[4,1024,256]{1,0,2:T(4,128)(2,1)} %copy.41) | data formatting | bytes 4194304 | tf_op jit(solution)/shard_map/reshape;reshape | solution.py:65
  136.0 6.7 %fusion.37 = (bf16[4,256,64]{1,2,0:T(8,128)(2,1)S(1)}, f32[8,4,256,64]{2,3,1,0:T(8,128)S(1)}) fusion(bf16[8,512,4,256]{1,3,2,0:T(8,128)(2,1)} %bitcast.86, bf16[8,512,4,64]{1,0,3,2:T(8,128)(2,1)} %reshape_reshape.10), kind=kOutput, calls=%fused_computation.60 | convolution fusion | flops 537329664 | bytes 12713984 | tf_op jit(solution)/shard_map/nbhf,nbhe->nhfe/dot_general | solution.py:68
  142.8 2.2 fusion.38
  145.3 20.9 %all-gather = bf16[16,256,64]{1,2,0:T(8,128)(2,1)} all-gather(bf16[4,256,64]{1,2,0:T(8,128)(2,1)S(1)} %get-tuple-element.203), channel_id=2, replica_groups=mesh['chain'=4,'ctx'=4,'tp'=2] {'chain'}, dimensions={0}, use_global_device_ids=true | all-gather | bytes 655360 | tf_op jit(solution)/shard_map/all_gather | solution.py:25
  166.2 10.2 %all-gather.1 = bf16[16,16,64]{2,1,0:T(8,128)(2,1)S(1)} all-gather(bf16[4,16,64]{2,1,0:T(8,128)(2,1)S(1)} %get-tuple-element.205), channel_id=3, replica_groups=mesh['chain'=4,'ctx'=4,'tp'=2] {'chain'}, dimensions={0}, use_global_device_ids=true | all-gather | bytes 40960 | tf_op jit(solution)/shard_map/all_gather | solution.py:25
  176.5 2.0 reduce_sum.50
  178.5 9.0 %all_gather.17 = bf16[4,4,64]{2,1,0:T(4,128)(2,1)S(1)} all-gather(bf16[1,4,64]{2,1,0:T(4,128)(2,1)S(1)} %all_gather.16), channel_id=1, replica_groups=mesh['chain'=4,'ctx'=4,'tp'=2] {'chain'}, dimensions={0}, use_global_device_ids=true | all-gather | bytes 2560 | tf_op jit(solution)/shard_map/all_gather | solution.py:25
  187.5 5.8 %while.18 = (s32[]{:T(128)}, f32[4,256,64]{2,1,0:T(8,128)S(1)}, f32[4,16,64]{2,1,0:T(8,128)S(1)}, f32[4,64]{1,0:T(4,128)S(1)}, s32[]{:T(128)}, /*index=5*/bf16[4...) while((s32[]{:T(128)}, f32[4,256,64]{2,1,0:T(8,128)S(1)}, ...), condition=%wide.region_5.6_spmd.clone, body=%wide.region_4.5_spmd.clone.sunk | while | flops 279556 | bytes 1223305 | solution.py:40
  187.5 0.9 constant_dynamic-slice_fusion.2
  189.0 0.9 constant_dynamic-slice_fusion.2
  190.4 0.9 constant_dynamic-slice_fusion.2
  191.9 0.9 constant_dynamic-slice_fusion.2
  193.5 1.5 fusion.39
  195.0 0.7 reduce_window_sum.35
  195.9 10.6 %fusion.17 = f32[8,4,64,512]{3,2,1,0:T(8,128)} fusion(bf16[8,512,4,256]{1,3,2,0:T(8,128)(2,1)} %bitcast.84, f32[8,4,256,64]{2,3,1,0:T(8,128)} %fusion.39, f32[8,4,256,64]{2,3,1,0:T(8,128)S(1)} %get-tuple-element.204, f32[4,256,64]{1,2,0:T(8,128)S(1)} %copy.47), kind=kOutput, calls=%fused_computation.33 | convolution fusion | flops 3222274048 | bytes 17039360 | tf_op jit(solution)/shard_map/nbhf,nhfe->nbhe/dot_general | solution.py:89
  206.6 17.6 %fusion = f32[8,4,64,512]{3,2,1,0:T(8,128)} fusion(f32[8,4,512,512]{3,2,1,0:T(8,128)} %fusion.40, pred[512,512]{1,0:T(8,128)(4,1)} %iota_compare_fusion, bf16[8,512,4,64]{1,0,3,2:T(8,128)(2,1)} %reshape_reshape.10, bf16[8,512,4,16]{1,0,3,2:T(8,128)(2,1)S(1)} %copy-done.6, bf16[8,512,4,16]{1,0,3,2:T(8,128)(2,1)} %copy-done.7), kind=kOutput, calls=%fused_computation.7 | convolution fusion | flops 1384120320 | bytes 41156608 | tf_op jit(solution)/shard_map/nhbc,nche->nbhe/dot_general | solution.py:108
  224.2 6.4 %multiply_reduce_fusion = (f32[8,512,4]{1,2,0:T(4,128)S(1)}, f32[8,512,4,64]{1,3,2,0:T(8,128)}) fusion(f32[8,4,64,512]{3,2,1,0:T(8,128)} %fusion, f32[8,4,64]{2,1,0:T(4,128)S(1)} %copy.53, f32[8,4,64,512]{3,2,1,0:T(8,128)} %fusion.17, f32[8,4,16,64]{3,2,1,0:T(8,128)S(1)} %fusion.25, bf16[8,512,4,16]{1,0,3,2:T(8,128)(2,1)S(1)} %copy-done.6), kind=kOutput, calls=%fused_computation.27 | convolution fusion | flops 207601664 | bytes 13312000 | tf_op jit(solution)/shard_map/nbhf,nhfe->nbhe/dot_general | solution.py:90
  230.7 2.4 mul.146
  233.1 6.2 %mul.147 = f32[4,1024,256]{1,0,2:T(4,128)} reshape(f32[4096,4,64]{0,2,1:T(8,128)} %mul.146) | data formatting | bytes 8388608 | tf_op jit(solution)/shard_map/mul | solution.py:115
  239.4 6.6 %copy.59 = f32[8,512,4,64]{1,0,3,2:T(8,128)} copy(f32[8,512,4,64]{1,3,2,0:T(8,128)} %get-tuple-element.208) | data formatting | bytes 8388608 | tf_op jit(solution)/shard_map/add | solution.py:109
  245.9 5.9 %reshape.178 = f32[4,1024,256]{1,0,2:T(4,128)} reshape(f32[8,512,4,64]{1,0,3,2:T(8,128)} %copy.59) | data formatting | bytes 8388608 | tf_op jit(solution)/shard_map/reshape | solution.py:110
  251.9 5.7 %multiply_convert_fusion.2 = bf16[4,1024,256]{1,0,2:T(4,128)(2,1)S(1)} fusion(f32[4,1024,256]{1,0,2:T(4,128)} %reshape.178, f32[4,1024,256]{1,0,2:T(4,128)} %mul.147), kind=kLoop, calls=%fused_computation.26 | loop fusion | flops 2097152 | bytes 10485760 | tf_op jit(solution)/shard_map/convert_element_type | solution.py:115
  257.6 0.6 copy.60
  258.2 19.7 %all_to_all.58 = bf16[4,1024,256]{1,2,0:T(8,128)(2,1)S(1)} all-to-all(bf16[4,1024,256]{1,2,0:T(8,128)(2,1)S(1)} %copy.60), channel_id=1, replica_groups=mesh['chain'=4,'ctx'=4,'tp'=2] {'ctx'}, dimensions={0} | all-to-all | bytes 4194304 | tf_op jit(solution)/shard_map/all_to_all | solution.py:154
  278.0 2.4 fusion.12
  280.4 6.3 %fusion.13 = bf16[1024,2048]{1,0:T(8,128)(2,1)} fusion(bf16[1,1024,2048]{2,1,0:T(8,128)(2,1)S(1)} %copy-done.14, bf16[1024,1,1024]{0,2,1:T(8,128)(2,1)S(1)} %fusion.12), kind=kOutput, calls=%fused_computation.31 | convolution fusion | flops 4297064448 | bytes 10485760 | tf_op jit(solution)/shard_map/dot_general | solution.py:162
  286.7 19.6 %reduce-scatter.2.cloned.1.call-done = bf16[512,2048]{1,0:T(8,128)(2,1)} async-done(((bf16[1024,2048]{1,0:T(8,128)(2,1)}), bf16[512,2048]{1,0:T(8,128)(2,1)}) %reduce-scatter.2.cloned.1.call-update) | async-done | bytes 2097168 | tf_op jit(solution)/shard_map/reduce_scatter | solution.py:161
  (75 shorter events, 4.2 us)
Async XLA Ops:
  6.5 39.4 %copy-start = (bf16[2048,256]{1,0:T(8,128)(2,1)S(1)}, bf16[2048,256]{1,0:T(8,128)(2,1)}, u32[]{:S(2)}) copy-start(bf16[2048,256]{1,0:T(8,128)(2,1)} %param.13) | copy-start | bytes 3145732
  23.6 22.4 %copy-start.13 = (bf16[1024,2048]{1,0:T(8,128)(2,1)S(1)}, bf16[1024,2048]{1,0:T(8,128)(2,1)}, u32[]{:S(2)}) copy-start(bf16[1024,2048]{1,0:T(8,128)(2,1)} %param.9) | copy-start | bytes 12582916
  41.7 6.4 %copy-start.5 = (bf16[1024,3072]{1,0:T(8,128)(2,1)}, bf16[1024,3072]{1,0:T(8,128)(2,1)S(1)}, u32[]{:S(2)}) copy-start(bf16[1024,3072]{1,0:T(8,128)(2,1)S(1)} %convolution_convert_fusion) | copy-start | bytes 18874372
  41.7 9.9 %copy-start.11 = (f32[3,3,1,1024]{3,2,1,0:T(1,128)S(1)}, f32[3,3,1,1024]{3,2,1,0:T(1,128)}, u32[]{:S(2)}) copy-start(f32[3,3,1,1024]{3,2,1,0:T(1,128)} %param.11) | copy-start | bytes 110596
  41.7 9.9 %copy-start.15 = (bf16[2048,256]{1,0:T(8,128)(2,1)S(1)}, bf16[2048,256]{1,0:T(8,128)(2,1)}, u32[]{:S(2)}) copy-start(bf16[2048,256]{1,0:T(8,128)(2,1)} %param.12) | copy-start | bytes 3145732
  41.8 23.7 %collective-permute-start = (bf16[2,3,1024]{2,0,1:T(2,128)(2,1)S(1)}, bf16[2,3,1024]{2,0,1:T(2,128)(2,1)S(1)}, u32[]{:S(2)}, u32[]{:S(2)}) collective-permute-start(bf16[2,3,1024]{2,0,1:T(2,128)(2,1)S(1)} %bitcast.99), channel_id=1, source_target_pairs={{0,2},{2,4},{4,6},{6,8},{8,10},{10,12},{12,14},{14,16},{16,18},{18... | collective-permute-start | bytes 36872 | tf_op jit(solution)/shard_map/ppermute | solution.py:19
  48.1 36.1 %all-to-all-start = ((bf16[1024,4,64]{0,2,1:T(8,128)(2,1)}), bf16[1024,4,64]{0,2,1:T(8,128)(2,1)S(1)}, u32[]{:S(2)}, u32[]{:S(2)}) async-start(bf16[1024,4,64]{0,2,1:T(8,128)(2,1)} %bitcast.3), calls=%async_computation | async-start | bytes 1048576 | tf_op jit(solution)/shard_map/all_to_all | solution.py:140
  80.2 2.6 copy-start.2
  84.2 10.9 %all-to-all-start.2 = ((bf16[1024,4,64]{0,2,1:T(8,128)(2,1)}), bf16[1024,4,64]{0,2,1:T(8,128)(2,1)S(1)}, u32[]{:S(2)}, u32[]{:S(2)}) async-start(bf16[1024,4,64]{0,2,1:T(8,128)(2,1)} %bitcast.10), calls=%async_computation.2 | async-start | bytes 1048576 | tf_op jit(solution)/shard_map/all_to_all | solution.py:139
  88.6 6.5 %copy-start.7 = (bf16[8,512,4,16]{1,0,3,2:T(8,128)(2,1)}, bf16[8,512,4,16]{1,0,3,2:T(8,128)(2,1)S(1)}, u32[]{:S(2)}) copy-start(bf16[8,512,4,16]{1,0,3,2:T(8,128)(2,1)S(1)} %reshape_reshape.9) | copy-start | bytes 1572868
  95.1 0.8 copy-start.9
  95.9 33.2 %all-to-all-start.1 = ((bf16[1024,4,256]{0,2,1:T(8,128)(2,1)}), bf16[1024,4,256]{0,2,1:T(8,128)(2,1)S(1)}, u32[]{:S(2)}, u32[]{:S(2)}) async-start(bf16[1024,4,256]{0,2,1:T(8,128)(2,1)} %bitcast.92), calls=%async_computation.1 | async-start | bytes 4194304 | tf_op jit(solution)/shard_map/all_to_all | solution.py:141
  99.5 206.8 %reduce-scatter.2.cloned.1.call-start = ((), (), s32[]{:S(2)}) async-start(), calls=%async_computation.5 | async-start | bytes 6291456 | tf_op jit(solution)/shard_map/reduce_scatter | solution.py:161
  129.0 2.9 copy-start.4
  136.0 6.8 %copy-start.3 = (bf16[8,512,4,64]{1,0,3,2:T(8,128)(2,1)S(1)}, bf16[8,512,4,64]{1,0,3,2:T(8,128)(2,1)}, u32[]{:S(2)}) copy-start(bf16[8,512,4,64]{1,0,3,2:T(8,128)(2,1)} %reshape_reshape.10) | copy-start | bytes 6291460
  136.0 6.8 %copy-start.8 = (bf16[8,512,4,16]{1,0,3,2:T(8,128)(2,1)S(1)}, bf16[8,512,4,16]{1,0,3,2:T(8,128)(2,1)}, u32[]{:S(2)}) copy-start(bf16[8,512,4,16]{1,0,3,2:T(8,128)(2,1)} %copy-done.7) | copy-start | bytes 1572868
  195.9 10.6 %copy-start.10 = (f32[8,4,16,64]{3,2,1,0:T(8,128)S(1)}, f32[8,4,16,64]{3,2,1,0:T(8,128)}, u32[]{:S(2)}) copy-start(f32[8,4,16,64]{3,2,1,0:T(8,128)} %get-tuple-element.206) | copy-start | bytes 393220
  195.9 10.7 %copy-start.6 = (bf16[8,512,4,16]{1,0,3,2:T(8,128)(2,1)S(1)}, bf16[8,512,4,16]{1,0,3,2:T(8,128)(2,1)}, u32[]{:S(2)}) copy-start(bf16[8,512,4,16]{1,0,3,2:T(8,128)(2,1)} %reshape_reshape.11) | copy-start | bytes 1572868
  245.9 32.0 %slice-start = ((s8[6291456]{0:T(1024)(128)(4,1)}), s8[2097152]{0:T(1024)(128)(4,1)S(1)}, s32[]{:S(2)}) async-start(s8[6291456]{0:T(1024)(128)(4,1)} %bitcast.87), calls=%async_computation.6 | async-start | bytes 4194304
  251.9 26.1 %slice-start.1 = ((s8[6291456]{0:T(1024)(128)(4,1)}), s8[4194304]{0:T(1024)(128)(4,1)S(1)}, s32[]{:S(2)}) async-start(s8[6291456]{0:T(1024)(128)(4,1)} %bitcast.87), calls=%async_computation.7 | async-start | bytes 8388608
  257.5 20.4 %copy-start.12 = (f32[1,1024]{1,0:T(1,128)S(1)}, f32[1,1024]{1,0:T(1,128)}, u32[]{:S(2)}) copy-start(f32[1,1024]{1,0:T(1,128)} %param.14) | copy-start | bytes 12292
  278.0 2.5 copy-start.14
  280.4 25.9 %copy-start.1 = (bf16[2048,256]{1,0:T(8,128)(2,1)S(1)}, bf16[2048,256]{1,0:T(8,128)(2,1)}, u32[]{:S(2)}) copy-start(bf16[2048,256]{1,0:T(8,128)(2,1)} %param.13) | copy-start | bytes 3145732
Sparse Core Ops, SparseCore 0:
  286.9 19.3 reduce-scatter.1
where the time goes:
time: 319 us; the launch traced here: 313 us
  matrix products  92.2 us (29%)
  local copies, waits for them, and re-layouts  70.7 us (22%)
  blocking collectives  59.9 us (19%)
  other arithmetic  41.7 us (13%)
  waiting for transfers between devices  19.6 us (6%)
  starting transfers between devices  15.2 us (5%)
  between operations  14 us (4%)
    all_gather x3, blocking collectives, prefix_2(): lax.all_gather(part.astype(kind), axis)  40.1 us
    unnamed x39, local copies, waits for them, and re-layouts  20.5 us
    all_to_all x1, blocking collectives, per_device(): lax.all_to_all(normed, 'ctx', split_axis=0, concat_axis=1, tiled=True)  19.7 us
    reduce_scatter x1, waiting for transfers between devices, per_device(): lax.psum_scatter(jnp.dot(mixed, out_weight, preferred_element_type=jnp.fl...  19.6 us
    dot_general x1, matrix products, per_device(): jnp.dot(tokens, w_in.reshape(width, 3 * half_width), preferred_element_ty...  18.1 us
    dot_general x1, matrix products, finish_blocks(): jnp.einsum('nbhf,nchf->nhbc', qwide_blocks, kwide_blocks, preferred_eleme...  17.8 us
    dot_general x1, matrix products, finish_blocks(): jnp.einsum('nhbc,nche->nbhe', kernel, value_blocks, preferred_element_typ...  17.6 us
    convert_element_type x1, other arithmetic, per_device(): convolved = (filters[0] * extended[2:].astype(jnp.float32) + filters[1] *...  14.3 us
  transfers between devices with their start and end apart: 5, of which 1 were waited for; matrix products, arithmetic and copies ran while one was open for 22% of the time, Pallas kernels for 0%

commit v1 on v0

v1 whole, which is shorter than its diff:
```python
import functools

import jax
import jax.numpy as jnp
from jax import lax
from jax.experimental import pallas as pl
from jax.experimental.pallas import tpu as pltpu
from jax.sharding import PartitionSpec as P

H = 16
F = 16
EPS = 1e-05
CHUNK = 256
GROUPS = 4
PER = H // GROUPS
SLABS = 10
ROWS = SLABS * F
WIDE = SLABS * PER * F
F32 = jnp.float32
BF16 = jnp.bfloat16
MIB = 1 << 20


def params(mib):
    return pltpu.CompilerParams(vmem_limit_bytes=mib * MIB, dimension_semantics=("arbitrary",))


def dot(a, b):
    return jnp.dot(a, b, preferred_element_type=F32)


def lanes(shape):
    return lax.broadcasted_iota(jnp.int32, shape, len(shape) - 1)


def qk_body(x, wq, wk, q_out, kt_out):
    q_out[...] = dot(x[...], wq[...]).astype(BF16)
    keys = dot(x[...], wk[...]).astype(BF16).astype(F32)
    kt_out[...] = keys.T.astype(BF16)


def project_qk(tokens, w_q, w_k):
    rows, width = tokens.shape
    feats = w_q.shape[1]
    return pl.pallas_call(
        qk_body,
        grid=(rows // CHUNK,),
        in_specs=[
            pl.BlockSpec((CHUNK, width), lambda c: (c, 0)),
            pl.BlockSpec((width, feats), lambda c: (0, 0)),
            pl.BlockSpec((width, feats), lambda c: (0, 0)),
        ],
        out_specs=[
            pl.BlockSpec((CHUNK, feats), lambda c: (c, 0)),
            pl.BlockSpec((feats, CHUNK), lambda c: (0, c)),
        ],
        out_shape=[
            jax.ShapeDtypeStruct((rows, feats), BF16),
            jax.ShapeDtypeStruct((feats, rows), BF16),
        ],
        compiler_params=params(24),
        name="project_qk",
    )(tokens, w_q, w_k)


def convolve(c, halo, x, w, taps, stream, hold):
    @pl.when(c == 0)
    def _():
        hold[0:8] = dot(halo[...], w).astype(BF16).astype(F32)

    @pl.when(c > 0)
    def _():
        hold[0:8] = hold[CHUNK : CHUNK + 8]

    hold[8 : CHUNK + 8] = dot(x[...], w).astype(BF16).astype(F32)
    return (
        taps[0, stream] * hold[8 : CHUNK + 8]
        + taps[1, stream] * hold[7 : CHUNK + 7]
        + taps[2, stream] * hold[6 : CHUNK + 6]
    ).astype(BF16)


def key_features(kt, dup, g):
    own = kt[g * 64 : (g + 1) * 64].astype(F32).reshape(PER, F, CHUNK)
    slabs = []
    for r in range(8):
        slabs.append((own * dup[g * PER : (g + 1) * PER, r : r + F]).astype(BF16))
    row = lax.broadcasted_iota(jnp.int32, own.shape, 1)
    last = jnp.where(row < 8, own * dup[g * PER : (g + 1) * PER, 8 : 8 + F], 0.0)
    slabs.append(jnp.where(row == 8, 1.0, last).astype(BF16))
    slabs.append(own.astype(BF16))
    return jnp.concatenate([s.reshape(PER * F, CHUNK) for s in slabs], axis=0)


def values_body(place, halo, x, w, taps, kt, v_out, before_out, *rest):
    pieces = rest[:-4]
    hold, dup, acc, flat = rest[-4:]
    c = pl.program_id(0)
    values = convolve(c, halo, x, w[0], taps, 0, hold)
    v_out[...] = values

    @pl.when(c == 0)
    def _():
        acc[...] = jnp.zeros_like(acc)

    before_out[0] = acc[...].astype(BF16)
    whole = kt[...].astype(F32).reshape(H, F, CHUNK)
    dup[:, 0:F] = whole
    dup[:, F : 2 * F] = whole
    low = lanes((SLABS, F, 128)) < 64
    for g in range(GROUPS):
        state = dot(key_features(kt, dup, g), values[:, g * 256 : (g + 1) * 256])
        state = state.reshape(SLABS, PER, F, 256)
        left = jnp.where(low, state[:, 0, :, :128], state[:, 1, :, :128])
        right = jnp.where(low, state[:, 2, :, 128:], state[:, 3, :, 128:])
        acc[g, :, :128] += left.reshape(ROWS, 128)
        acc[g, :, 128:] += right.reshape(ROWS, 128)

    @pl.when(c == pl.num_programs(0) - 1)
    def _():
        n = len(pieces)
        flat[...] = acc[...].reshape(n, GROUPS * ROWS // n, 256).astype(BF16)
        for m, piece in enumerate(pieces):
            piece[...] = flat[lax.rem(place[0] + m, n)]


def project_values(place, halo, tokens, w, taps, kt, n):
    rows, width = tokens.shape
    half = w.shape[2]
    part = GROUPS * ROWS // n
    return pl.pallas_call(
        values_body,
        grid_spec=pltpu.PrefetchScalarGridSpec(
            num_scalar_prefetch=1,
            grid=(rows // CHUNK,),
            in_specs=[
                pl.BlockSpec((8, width), lambda c, s: (0, 0)),
                pl.BlockSpec((CHUNK, width), lambda c, s: (c, 0)),
                pl.BlockSpec((1, width, half), lambda c, s: (0, 0, 0)),
                pl.BlockSpec((3, 3, half), lambda c, s: (0, 0, 0)),
                pl.BlockSpec((H * F, CHUNK), lambda c, s: (0, c)),
            ],
            out_specs=[
                pl.BlockSpec((CHUNK, half), lambda c, s: (c, 0)),
                pl.BlockSpec((1, GROUPS, ROWS, 256), lambda c, s: (c, 0, 0, 0)),
            ]
            + [pl.BlockSpec((part, 256), lambda c, s: (0, 0)) for _ in range(n)],
            scratch_shapes=[
                pltpu.VMEM((CHUNK + 8, half), F32),
                pltpu.VMEM((H, 2 * F, CHUNK), F32),
                pltpu.VMEM((GROUPS, ROWS, 256), F32),
                pltpu.VMEM((n, part, 256), BF16),
            ],
        ),
        out_shape=[
            jax.ShapeDtypeStruct((rows, half), BF16),
            jax.ShapeDtypeStruct((rows // CHUNK, GROUPS, ROWS, 256), BF16),
        ]
        + [jax.ShapeDtypeStruct((part, 256), BF16) for _ in range(n)],
        compiler_params=params(40),
        name="project_values",
    )(place, halo, tokens, w, taps, kt)


def stream_body(stream, halo, x, w, taps, out, hold):
    out[...] = convolve(pl.program_id(0), halo, x, w[0], taps, stream, hold)


def project_stream(stream, halo, tokens, w, taps):
    rows, width = tokens.shape
    half = w.shape[2]
    return pl.pallas_call(
        functools.partial(stream_body, stream),
        grid=(rows // CHUNK,),
        in_specs=[
            pl.BlockSpec((8, width), lambda c: (0, 0)),
            pl.BlockSpec((CHUNK, width), lambda c: (c, 0)),
            pl.BlockSpec((1, width, half), lambda c: (stream, 0, 0)),
            pl.BlockSpec((3, 3, half), lambda c: (0, 0, 0)),
        ],
        out_specs=pl.BlockSpec((CHUNK, half), lambda c: (c, 0)),
        out_shape=jax.ShapeDtypeStruct((rows, half), BF16),
        scratch_shapes=[pltpu.VMEM((CHUNK + 8, half), F32)],
        compiler_params=params(32),
        name="project_gate" if stream == 1 else "project_skip",
    )(halo, tokens, w, taps)


def inside_body(place, q, kt, v, out):
    low = lanes((CHUNK, 128)) < 64
    head = lanes((CHUNK, 128)) // F
    causal = lax.broadcasted_iota(jnp.int32, (CHUNK, CHUNK), 0) >= lanes((CHUNK, CHUNK))
    for part in range(2):
        query = q[:, part * 128 : (part + 1) * 128] * 0.25
        stacked = jnp.concatenate(
            [jnp.where(head == h, query, 0.0).astype(BF16) for h in range(8)], axis=0
        )
        score = dot(stacked, kt[part * 128 : (part + 1) * 128])
        for pair in range(4):
            both = []
            at = part * 512 + pair * 128
            for h in (2 * pair, 2 * pair + 1):
                x = score[h * CHUNK : (h + 1) * CHUNK]
                poly = x * (0.5 * x + 1.0) + 1.0
                weight = jnp.where(causal, poly, 0.0).astype(BF16)
                both.append(dot(weight, v[:, at : at + 128]))
            out[:, at : at + 128] = jnp.where(low, both[0], both[1])


def inside(place, q, kt, v, count, start):
    half = v.shape[1]
    return pl.pallas_call(
        inside_body,
        grid_spec=pltpu.PrefetchScalarGridSpec(
            num_scalar_prefetch=1,
            grid=(count,),
            in_specs=[
                pl.BlockSpec((CHUNK, H * F), lambda c, s: (s[start] + c, 0)),
                pl.BlockSpec((H * F, CHUNK), lambda c, s: (0, s[start] + c)),
                pl.BlockSpec((CHUNK, half), lambda c, s: (s[start] + c, 0)),
            ],
            out_specs=pl.BlockSpec((CHUNK, half), lambda c, s: (c, 0)),
        ),
        out_shape=jax.ShapeDtypeStruct((count * CHUNK, half), F32),
        compiler_params=params(24),
        name="inside",
    )(place, q, kt, v)


def spread():
    src = lax.broadcasted_iota(jnp.int32, (H * F, GROUPS * WIDE), 0)
    col = lax.broadcasted_iota(jnp.int32, (H * F, GROUPS * WIDE), 1)
    g, rest = col // WIDE, col % WIDE
    slab, h, i = rest // 64, (rest // F) % PER, rest % F
    shift = jnp.where(slab == 9, 0, slab)
    want = g * 64 + h * F + (i + shift) % F
    scale = jnp.where(slab == 0, 1.0 / 32, jnp.where(slab == 9, 0.25, 1.0 / 16))
    scale = jnp.where((slab == 8) & (i >= 8), 0.0, scale)
    second = jnp.where(src == want, scale, 0.0).astype(BF16)
    src = lax.broadcasted_iota(jnp.int32, (H * F, GROUPS * 128), 0)
    col = lax.broadcasted_iota(jnp.int32, (H * F, GROUPS * 128), 1)
    first = jnp.where(src == (col // 128) * 64 + col % 64, 1.0, 0.0).astype(BF16)
    return first, second


def finish_body(place, q, att, before, gate, skip, gain, w_o, first, second, *rest):
    pieces, (out, start, mixed) = rest[:-3], rest[-3:]
    n = len(pieces)

    @pl.when(pl.program_id(0) == 0)
    def _():
        for m, piece in enumerate(pieces):
            start[lax.rem(place[0] + n - m, n)] = piece[...]

    prefix = start[...].reshape(GROUPS, ROWS, 256).astype(F32)
    lane = lanes((CHUNK, 128))
    one = jnp.where((lane < 64) & (lane % F == 8), 1.0, 0.0)
    wide = lanes((SLABS, F, 256)) // 64
    mean = (lax.broadcasted_iota(jnp.int32, (256, 256), 0) // 64 == lanes((256, 256)) // 64)
    mean = jnp.where(mean, 1.0 / 64, 0.0).astype(BF16)
    lead = dot(q[...], first[...])
    for g in range(GROUPS):
        b = dot(q[...], second[:, g * WIDE : (g + 1) * WIDE])
        a = lead[:, g * 128 : (g + 1) * 128]
        feats = [(a * b[:, s * 128 : (s + 1) * 128]).astype(BF16) for s in range(4)]
        b4 = b[:, 512:640]
        feats.append((jnp.where(lane < 64, a * b4, b4) + one).astype(BF16))
        state = (prefix[g] + before[0, g].astype(F32)).astype(BF16).reshape(SLABS, F, 256)
        state = jnp.stack([jnp.where(wide == h, state, 0.0).astype(BF16) for h in range(PER)], axis=1)
        state = state.reshape(WIDE, 256)
        at = slice(g * 256, (g + 1) * 256)
        whole = att[:, at] + dot(jnp.concatenate(feats, axis=1), state)
        mean_sq = dot((whole * whole).astype(BF16), mean)
        normed = (whole * lax.rsqrt(mean_sq + EPS)).astype(BF16).astype(F32)
        gates = gate[:, at].astype(F32)
        act = gates / (1.0 + jnp.exp(-gates))
        mixed[:, at] = (act * (normed * gain[:, at] + skip[:, at].astype(F32))).astype(BF16)
    out[...] = dot(mixed[...], w_o[...]).astype(BF16)


def finish(place, q, att, before, gate, skip, gain, w_o, first, second, pieces, count, start):
    half, width = w_o.shape
    n = len(pieces)
    part = GROUPS * ROWS // n
    return pl.pallas_call(
        finish_body,
        grid_spec=pltpu.PrefetchScalarGridSpec(
            num_scalar_prefetch=1,
            grid=(count,),
            in_specs=[
                pl.BlockSpec((CHUNK, H * F), lambda c, s: (s[start] + c, 0)),
                pl.BlockSpec((CHUNK, half), lambda c, s: (s[start] + c, 0)),
                pl.BlockSpec((1, GROUPS, ROWS, 256), lambda c, s: (s[start] + c, 0, 0, 0)),
                pl.BlockSpec((CHUNK, half), lambda c, s: (s[start] + c, 0)),
                pl.BlockSpec((CHUNK, half), lambda c, s: (s[start] + c, 0)),
                pl.BlockSpec((1, half), lambda c, s: (0, 0)),
                pl.BlockSpec((half, width), lambda c, s: (0, 0)),
                pl.BlockSpec((H * F, GROUPS * 128), lambda c, s: (0, 0)),
                pl.BlockSpec((H * F, GROUPS * WIDE), lambda c, s: (0, 0)),
            ]
            + [pl.BlockSpec((part, 256), lambda c, s: (0, 0)) for _ in range(n)],
            out_specs=pl.BlockSpec((CHUNK, width), lambda c, s: (c, 0)),
            scratch_shapes=[
                pltpu.VMEM((n, part, 256), BF16),
                pltpu.VMEM((CHUNK, half), BF16),
            ],
        ),
        out_shape=jax.ShapeDtypeStruct((count * CHUNK, width), BF16),
        compiler_params=params(40),
        name="finish",
    )(place, q, att, before, gate, skip, gain, w_o, first, second, *pieces)


def shift(block, axes, distance, size):
    return lax.ppermute(block, axes, [(i, i + distance) for i in range(size - distance)])


def turn(block, axis, distance, size):
    return lax.ppermute(block, axis, [(i, (i + distance) % size) for i in range(size)])


def per_device(tokens, w_in, conv_w, w_q, w_k, gain, w_o):
    rows, width = tokens.shape
    half = w_in.shape[3]
    n, blocks = lax.axis_size("ctx"), lax.axis_size("chain")
    me, core = lax.axis_index("ctx"), lax.axis_index("tp")
    chunks = rows // CHUNK
    per_half = chunks // 2
    place = jnp.stack([me, (1 - core) * per_half, core * per_half, 0 * me]).astype(jnp.int32)
    streams = w_in.transpose(1, 2, 0, 3).reshape(3, width, half)
    taps = conv_w.reshape(3, 3, half)
    weight = w_o.reshape(half, width)

    halo = shift(tokens[rows - 8 :], ("chain", "ctx"), 1, n * blocks)
    q, kt = project_qk(tokens, w_q, w_k)
    values, before, *mine = project_values(place, halo, tokens, streams, taps, kt, n)
    theirs = [mine[0]] + [turn(mine[m], "ctx", m, n) for m in range(1, n)]
    gate = project_stream(1, halo, tokens, streams, taps)
    wide = [t.astype(F32) for t in theirs]
    total = sum(wide).astype(BF16)
    earlier = [shift(total, "chain", d, blocks) for d in range(1, blocks)]
    skip = project_stream(2, halo, tokens, streams, taps)
    base = sum(e.astype(F32) for e in earlier)
    starts = []
    for m in range(n):
        peer = (me + m) % n
        found = base
        for k, part in enumerate(wide):
            found = found + jnp.where((me - k) % n < peer, part, 0.0)
        starts.append(found.astype(BF16))
    got = [starts[0]] + [turn(starts[m], "ctx", m, n) for m in range(1, n)]
    att = inside(place, q, kt, values, chunks, 3)
    first, second = spread()
    tail = (q, att, before, gate, skip, gain, weight, first, second, got, per_half)
    away = finish(place, *tail, 1)
    swapped = lax.ppermute(away, "tp", [(0, 1), (1, 0)])
    home = finish(place, *tail, 2)
    return (home.astype(F32) + swapped.astype(F32)).astype(BF16)


def solution(mesh):
    return jax.shard_map(
        per_device,
        mesh=mesh,
        in_specs=(
            P(("chain", "ctx"), None),
            P(None, None, "tp", None),
            P(None, None, "tp", None),
            P(),
            P(),
            P("tp", None),
            P("tp", None, None),
        ),
        out_specs=P(("chain", "ctx", "tp"), None),
        check_vma=False,
    )
```

time: 319 us -> 109 us (0.34); the launches traced: 313 us -> 108 us
  matrix products: 92.2 us -> 0 us
  blocking collectives: 59.9 us -> 0 us
  Pallas kernels: 0 us -> 57.2 us
  local copies, waits for them, and re-layouts: 70.7 us -> 14.8 us
  other arithmetic: 41.7 us -> 6.53 us
  waiting for transfers between devices: 19.6 us -> 5.74 us
  between operations: 14 us -> 0.36 us
  starting transfers between devices: 15.2 us -> 23.9 us
    dot_general x10 -> x0, matrix products: 92.2 us -> none  [the longest x1 18.1 us: per_device(): jnp.dot(tokens, w_in.reshape(width, 3 * half_width), preferred_element_ty...]
    pallas_call x0 -> x7, Pallas kernels: none -> 57.2 us  [the longest x2 18.9 us: finish(): pl.pallas_call(finish_body, grid_spec=pltpu.PrefetchScalarGridSpec(num_sc...]
    all_gather x3 -> x0, blocking collectives: 40.1 us -> none  [prefix_2(): lax.all_gather(part.astype(kind), axis)]
    convert_element_type x5 -> x6, other arithmetic: 34.9 us -> 6.41 us  [the longest x2 2.22 us: per_device(): starts.append(found.astype(BF16))]
    all_to_all x1 -> x0, blocking collectives: 19.7 us -> none  [per_device(): lax.all_to_all(normed, 'ctx', split_axis=0, concat_axis=1, tiled=True)]
    ppermute x1 -> x11, starting transfers between devices: 4.21 us -> 23.9 us  [the longest x4 12.9 us: shift(): lax.ppermute(block, axes, [(i, i + distance) for i in range(size - distan...]
    reduce_scatter x1 -> x0, waiting for transfers between devices: 19.6 us -> none  [per_device(): lax.psum_scatter(jnp.dot(mixed, out_weight, preferred_element_type=jnp.fl...]
    all_to_all x3 -> x0, starting transfers between devices: 10.9 us -> none  [the longest x1 3.84 us: per_device(): lax.all_to_all(queries, 'ctx', split_axis=1, concat_axis=0, tiled=True)]
  transfers between devices with their start and end apart: 5 -> 11, of which waited for: 1 -> 4; matrix products, arithmetic and copies ran while one was open for 22% -> 3% of each run, Pallas kernels for 0% -> 32%
where the time goes in v1:
time: 109 us; the launch traced here: 108 us
  Pallas kernels  57.2 us (52%)
  starting transfers between devices  23.9 us (22%)
  local copies, waits for them, and re-layouts  14.8 us (14%)
  other arithmetic  6.53 us (6%)
  waiting for transfers between devices  5.74 us (5%)
    pallas_call x2, Pallas kernels, finish(): pl.pallas_call(finish_body, grid_spec=pltpu.PrefetchScalarGridSpec(num_sc...  18.9 us
    pallas_call x2, Pallas kernels, project_stream(): pl.pallas_call(functools.partial(stream_body, stream), grid=(rows // CHUN...  15.8 us
    unnamed x41, local copies, waits for them, and re-layouts  14 us
    pallas_call x1, Pallas kernels, project_values(): pl.pallas_call(values_body, grid_spec=pltpu.PrefetchScalarGridSpec(num_sc...  13.2 us
    ppermute x4, starting transfers between devices, shift(): lax.ppermute(block, axes, [(i, i + distance) for i in range(size - distan...  12.9 us
    ppermute x6, starting transfers between devices, turn(): lax.ppermute(block, axis, [(i, (i + distance) % size) for i in range(size)])  6.34 us
    pallas_call x1, Pallas kernels, inside(): pl.pallas_call(inside_body, grid_spec=pltpu.PrefetchScalarGridSpec(num_sc...  6.1 us
    ppermute x6, waiting for transfers between devices, turn(): lax.ppermute(block, axis, [(i, (i + distance) % size) for i in range(size)])  5.73 us
  transfers between devices with their start and end apart: 11, of which 4 were waited for; matrix products, arithmetic and copies ran while one was open for 3% of the time, Pallas kernels for 32%

profile of v1, /device:TPU:1, one launch (start us, length us, event | category | flops | bytes accessed | tf_op | source)
XLA Modules:
  0.0 108.4 jit_solution(17468904147086225758)
XLA Ops:
  0.0 0.8 slice.3
  0.8 3.9 %collective-permute-start = (bf16[8,2048]{1,0:T(8,128)(2,1)S(1)}, bf16[8,2048]{1,0:T(8,128)(2,1)S(1)}, u32[]{:S(2)}, u32[]{:S(2)}) collective-permute-start(bf16[8,2048]{1,0:T(8,128)(2,1)S(1)} %slice.3), channel_id=1, source_target_pairs={{0,2},{2,4},{4,6},{6,8},{8,10},{10,12},{12,14},{14,16},{16,18},{18... | collective-permute-start | bytes 98312 | tf_op jit(solution)/shard_map/ppermute | solution.py:315
  4.8 0.6 fusion.4.second
  5.4 0.1 pad_add_fusion.place
  5.5 0.8 copy.11
  6.3 0.0 copy-start.1
  6.3 2.2 %copy-done.1 = bf16[1024,2048]{1,0:T(8,128)(2,1)S(1)} copy-done((bf16[1024,2048]{1,0:T(8,128)(2,1)S(1)}, bf16[1024,2048]{1,0:T(8,128)(2,1)}, u32[]{:S(2)}) %copy-start.1) | copy-done | bytes 4194328
  8.5 1.2 %copy-done.9 = bf16[2048,256]{1,0:T(8,128)(2,1)S(1)} copy-done((bf16[2048,256]{1,0:T(8,128)(2,1)S(1)}, bf16[2048,256]{1,0:T(8,128)(2,1)}, u32[]{:S(2)}) %copy-start.9) | copy-done | bytes 1048600
  9.7 1.2 %copy-done.10 = bf16[2048,256]{1,0:T(8,128)(2,1)S(1)} copy-done((bf16[2048,256]{1,0:T(8,128)(2,1)S(1)}, bf16[2048,256]{1,0:T(8,128)(2,1)}, u32[]{:S(2)}) %copy-start.10) | copy-done | bytes 1048600
  10.9 3.2 %project_qk.1 = (bf16[1024,256]{1,0:T(8,128)(2,1)S(1)}, bf16[256,1024]{1,0:T(8,128)(2,1)S(1)}) custom-call(bf16[1024,2048]{1,0:T(8,128)(2,1)S(1)} %copy-done.1, bf16[2048,256]{1,0:T(8,128)(2,1)S(1)} %copy-done.9, bf16[2048,256]{1,0:T(8,128)(2,1)S(1)} %copy-done.10), custom_call_target="tpu_custom_call" | custom-call | tf_op jit(solution)/shard_map/project_qk/pallas_call | solution.py:45
  14.1 0.0 collective-permute-done.halo
  14.2 13.2 %project_values.1 = (bf16[1024,1024]{1,0:T(8,128)(2,1)S(1)}, bf16[4,4,160,256]{3,2,1,0:T(8,128)(2,1)S(1)}, bf16[160,256]{1,0:T(8,128)(2,1)S(1)}, bf16[160,256]{1...) custom-call(s32[4]{0:T(128)S(1)} %pad_add_fusion.place, ...), custom_call_target="tpu_custom_call" | custom-call | tf_op jit(solution)/shard_map/project_values/pallas_call | solution.py:131
  27.3 1.1 copy-done.4
  28.4 1.3 %copy-done.7 = bf16[1024,1024]{1,0:T(8,128)(2,1)} copy-done((bf16[1024,1024]{1,0:T(8,128)(2,1)}, bf16[1024,1024]{1,0:T(8,128)(2,1)S(1)}, u32[]{:S(2)}) %copy-start.7) | copy-done | bytes 2097176
  29.7 1.2 %collective-permute-start.1 = (bf16[160,256]{1,0:T(8,128)(2,1)S(1)}, bf16[160,256]{1,0:T(8,128)(2,1)S(1)}, u32[]{:S(2)}, u32[]{:S(2)}) collective-permute-start(bf16[160,256]{1,0:T(8,128)(2,1)S(1)} %get-tuple-element.18), channel_id=1, source_target_pairs={{0,2},{2,4},{4,6},{6,0},{1,3},{3,5},{5,7},{7,1},{8,10},{10,12},{12... | collective-permute-start | bytes 245768 | tf_op jit(solution)/shard_map/ppermute | solution.py:319
  31.0 1.2 %collective-permute-start.2 = (bf16[160,256]{1,0:T(8,128)(2,1)S(1)}, bf16[160,256]{1,0:T(8,128)(2,1)S(1)}, u32[]{:S(2)}, u32[]{:S(2)}) collective-permute-start(bf16[160,256]{1,0:T(8,128)(2,1)S(1)} %get-tuple-element.19), channel_id=1, source_target_pairs={{0,4},{2,6},{4,0},{6,2},{1,5},{3,7},{5,1},{7,3},{8,12},{10,14},{12... | collective-permute-start | bytes 245768 | tf_op jit(solution)/shard_map/ppermute | solution.py:319
  32.2 1.2 %collective-permute-start.3 = (bf16[160,256]{1,0:T(8,128)(2,1)S(1)}, bf16[160,256]{1,0:T(8,128)(2,1)S(1)}, u32[]{:S(2)}, u32[]{:S(2)}) collective-permute-start(bf16[160,256]{1,0:T(8,128)(2,1)S(1)} %get-tuple-element.20), channel_id=1, source_target_pairs={{0,6},{2,0},{4,2},{6,4},{1,7},{3,1},{5,3},{7,5},{8,14},{10,8},{12,... | collective-permute-start | bytes 245768 | tf_op jit(solution)/shard_map/ppermute | solution.py:319
  33.4 0.6 collective-permute-done.1
  34.0 1.5 %collective-permute-done.2 = bf16[160,256]{1,0:T(8,128)(2,1)S(1)} collective-permute-done((bf16[160,256]{1,0:T(8,128)(2,1)S(1)}, bf16[160,256]{1,0:T(8,128)(2,1)S(1)}, u32[]{:S(2)}, u32[]{:S(2)}) %collective-permute-start.2) | collective-permute-done | bytes 81952 | tf_op jit(solution)/shard_map/ppermute | solution.py:319
  35.5 1.0 collective-permute-done.3
  36.6 0.7 fusion.37
  37.3 4.9 %collective-permute-start.6 = (bf16[160,256]{1,0:T(8,128)(2,1)}, bf16[160,256]{1,0:T(8,128)(2,1)}, u32[]{:S(2)}, u32[]{:S(2)}) collective-permute-start(bf16[160,256]{1,0:T(8,128)(2,1)} %fusion.37), channel_id=1, source_target_pairs={{0,24},{1,25},{2,26},{3,27},{4,28},{5,29},{6,30},{7,31}} | collective-permute-start | bytes 245768 | tf_op jit(solution)/shard_map/ppermute | solution.py:315
  42.1 1.9 %collective-permute-start.5 = (bf16[160,256]{1,0:T(8,128)(2,1)}, bf16[160,256]{1,0:T(8,128)(2,1)}, u32[]{:S(2)}, u32[]{:S(2)}) collective-permute-start(bf16[160,256]{1,0:T(8,128)(2,1)} %fusion.37), channel_id=1, source_target_pairs={{0,16},{8,24},{1,17},{9,25},{2,18},{10,26},{3,19},{11,27},{4,20},{... | collective-permute-start | bytes 245768 | tf_op jit(solution)/shard_map/ppermute | solution.py:315
  44.0 2.2 %collective-permute-start.4 = (bf16[160,256]{1,0:T(8,128)(2,1)}, bf16[160,256]{1,0:T(8,128)(2,1)}, u32[]{:S(2)}, u32[]{:S(2)}) collective-permute-start(bf16[160,256]{1,0:T(8,128)(2,1)} %fusion.37), channel_id=1, source_target_pairs={{0,8},{8,16},{16,24},{1,9},{9,17},{17,25},{2,10},{10,18},{18,26},{... | collective-permute-start | bytes 245768 | tf_op jit(solution)/shard_map/ppermute | solution.py:315
  46.2 0.8 select_convert_fusion.first
  47.0 1.6 %copy-done.8 = bf16[1024,1024]{1,0:T(8,128)(2,1)S(1)} copy-done((bf16[1024,1024]{1,0:T(8,128)(2,1)S(1)}, bf16[1024,1024]{1,0:T(8,128)(2,1)}, u32[]{:S(2)}) %copy-start.8) | copy-done | bytes 2097176
  48.6 6.1 %inside.1.att = f32[1024,1024]{1,0:T(8,128)S(1)} custom-call(s32[4]{0:T(128)S(1)} %pad_add_fusion.place, bf16[1024,256]{1,0:T(8,128)(2,1)S(1)} %get-tuple-element.13.q, bf16[256,1024]{1,0:T(8,128)(2,1)S(1)} %get-tuple-element.14.kt, bf16[1024,1024]{1,0:T(8,128)(2,1)S(1)} %copy-done.8), custom_call_target="tpu_custom_call" | custom-call | tf_op jit(solution)/shard_map/inside/pallas_call | solution.py:212
  54.7 0.0 copy-start
  54.8 4.6 %copy-done = bf16[2048,3,1,1024]{3,0,2,1:T(8,128)(2,1)S(1)} copy-done((bf16[2048,3,1,1024]{3,0,2,1:T(8,128)(2,1)S(1)}, bf16[2048,3,1,1024]{3,0,2,1:T(8,128)(2,1)}, u32[]{:S(2)}) %copy-start) | copy-done | bytes 12582936
  59.3 7.9 %project_skip.1.skip = bf16[1024,1024]{1,0:T(8,128)(2,1)S(1)} custom-call(bf16[8,2048]{1,0:T(8,128)(2,1)S(1)} %collective-permute-done.halo, bf16[1024,2048]{1,0:T(8,128)(2,1)S(1)} %copy-done.3, bf16[3,2048,1024]{2,1,0:T(8,128)(2,1)S(1)} %bitcast.13, f32[3,3,1024]{2,1,0:T(4,128)S(1)} %bitcast.16), custom_call_target="tpu_custom_call" | custom-call | tf_op jit(solution)/shard_map/project_skip/pallas_call | solution.py:172
  67.3 0.0 copy-start.13
  67.3 7.9 %project_gate.1.gate = bf16[1024,1024]{1,0:T(8,128)(2,1)S(1)} custom-call(bf16[8,2048]{1,0:T(8,128)(2,1)S(1)} %collective-permute-done.halo, bf16[1024,2048]{1,0:T(8,128)(2,1)S(1)} %copy-done.3, bf16[3,2048,1024]{2,1,0:T(8,128)(2,1)S(1)} %bitcast.14, f32[3,3,1024]{2,1,0:T(4,128)S(1)} %bitcast.17), custom_call_target="tpu_custom_call" | custom-call | tf_op jit(solution)/shard_map/project_gate/pallas_call | solution.py:172
  75.2 0.0 collective-permute-done.6
  75.2 0.0 collective-permute-done.5
  75.3 0.0 collective-permute-done.4
  75.3 1.2 %fusion.32 = (bf16[160,256]{1,0:T(8,128)(2,1)S(1)}, bf16[160,256]{1,0:T(8,128)(2,1)S(1)}, bf16[160,256]{1,0:T(8,128)(2,1)S(1)}) fusion(bf16[160,256]{1,0:T(8,128)(2,1)S(1)} %copy-done.12, bf16[160,256]{1,0:T(8,128)(2,1)S(1)} %copy-done.15, bf16[160,256]{1,0:T(8,128)(2,1)S(1)} %copy-done.17, bf16[160,256]{1,0:T(8,128)(2,1)S(1)} %copy-done.19, pred[]{:T(512)S(6)} %lt.164, ...), kind=kLoop, calls=%fused_computation.72 | loop fusion | flops 1474560 | bytes 819212 | tf_op jit(solution)/shard_map/convert_element_type | solution.py:350
  76.5 2.1 %collective-permute-start.9 = (bf16[160,256]{1,0:T(8,128)(2,1)S(1)}, bf16[160,256]{1,0:T(8,128)(2,1)S(1)}, u32[]{:S(2)}, u32[]{:S(2)}) collective-permute-start(bf16[160,256]{1,0:T(8,128)(2,1)S(1)} %get-tuple-element.21), channel_id=1, source_target_pairs={{0,6},{2,0},{4,2},{6,4},{1,7},{3,1},{5,3},{7,5},{8,14},{10,8},{12,... | collective-permute-start | bytes 245768 | tf_op jit(solution)/shard_map/ppermute | solution.py:319
  78.6 0.0 collective-permute-start.7
  78.6 0.6 collective-permute-start.8
  79.2 1.1 fusion.36.rest_0_
  80.3 0.0 collective-permute-done.9.rest_3_
  80.3 2.5 %collective-permute-done.7.rest_1_ = bf16[160,256]{1,0:T(8,128)(2,1)S(1)} collective-permute-done((bf16[160,256]{1,0:T(8,128)(2,1)S(1)}, bf16[160,256]{1,0:T(8,128)(2,1)S(1)}, u32[]{:S(2)}, u32[]{:S(2)}) %collective-permute-start.7) | collective-permute-done | bytes 81952 | tf_op jit(solution)/shard_map/ppermute | solution.py:319
  82.8 0.0 collective-permute-done.8.rest_2_
  82.8 9.4 %finish.3 = bf16[512,2048]{1,0:T(8,128)(2,1)S(1)} custom-call(s32[4]{0:T(128)S(1)} %pad_add_fusion.place, bf16[1024,256]{1,0:T(8,128)(2,1)S(1)} %get-tuple-element.13.q, f32[1024,1024]{1,0:T(8,128)S(1)} %inside.1.att, bf16[4,4,160,256]{3,2,1,0:T(8,128)(2,1)S(1)} %copy-done.5, bf16[1024,1024]{1,0:T(8,128)(2,1)S(1)} %project_gate.1.gate, ...), custom_call_target="tpu_custom_call" | custom-call | tf_op jit(solution)/shard_map/finish/pallas_call | solution.py:285
  92.3 4.6 %collective-permute-start.10 = (bf16[512,2048]{1,0:T(8,128)(2,1)S(1)}, bf16[512,2048]{1,0:T(8,128)(2,1)S(1)}, u32[]{:S(2)}, u32[]{:S(2)}) collective-permute-start(bf16[512,2048]{1,0:T(8,128)(2,1)S(1)} %finish.3), channel_id=1, source_target_pairs={{0,1},{1,0},{2,3},{3,2},{4,5},{5,4},{6,7},{7,6},{8,9},{9,8},{10,11... | collective-permute-start | bytes 6291464 | tf_op jit(solution)/shard_map/ppermute | solution.py:356
  96.9 9.4 %finish.2 = bf16[512,2048]{1,0:T(8,128)(2,1)S(1)} custom-call(s32[4]{0:T(128)S(1)} %pad_add_fusion.place, bf16[1024,256]{1,0:T(8,128)(2,1)S(1)} %get-tuple-element.13.q, f32[1024,1024]{1,0:T(8,128)S(1)} %inside.1.att, bf16[4,4,160,256]{3,2,1,0:T(8,128)(2,1)S(1)} %copy-done.5, bf16[1024,1024]{1,0:T(8,128)(2,1)S(1)} %project_gate.1.gate, ...), custom_call_target="tpu_custom_call" | custom-call | tf_op jit(solution)/shard_map/finish/pallas_call | solution.py:285
  106.3 0.0 collective-permute-done.10
  106.3 2.1 %add_convert_fusion = bf16[512,2048]{1,0:T(8,128)(2,1)} fusion(bf16[512,2048]{1,0:T(8,128)(2,1)S(1)} %collective-permute-done.10, bf16[512,2048]{1,0:T(8,128)(2,1)S(1)} %finish.2), kind=kLoop, calls=%fused_computation.4 | loop fusion | flops 4194304 | bytes 6291456 | tf_op jit(solution)/shard_map/convert_element_type | solution.py:358
  (36 shorter events, 0.1 us)
Async XLA Ops:
  0.8 13.4 %collective-permute-start = (bf16[8,2048]{1,0:T(8,128)(2,1)S(1)}, bf16[8,2048]{1,0:T(8,128)(2,1)S(1)}, u32[]{:S(2)}, u32[]{:S(2)}) collective-permute-start(bf16[8,2048]{1,0:T(8,128)(2,1)S(1)} %slice.3), channel_id=1, source_target_pairs={{0,2},{2,4},{4,6},{6,8},{8,10},{10,12},{12,14},{14,16},{16,18},{18... | collective-permute-start | bytes 98312 | tf_op jit(solution)/shard_map/ppermute | solution.py:315
  6.3 2.2 %copy-start.1 = (bf16[1024,2048]{1,0:T(8,128)(2,1)S(1)}, bf16[1024,2048]{1,0:T(8,128)(2,1)}, u32[]{:S(2)}) copy-start(bf16[1024,2048]{1,0:T(8,128)(2,1)} %x.7) | copy-start | bytes 12582916
  8.5 1.2 %copy-start.9 = (bf16[2048,256]{1,0:T(8,128)(2,1)S(1)}, bf16[2048,256]{1,0:T(8,128)(2,1)}, u32[]{:S(2)}) copy-start(bf16[2048,256]{1,0:T(8,128)(2,1)} %wq.1) | copy-start | bytes 3145732
  9.7 1.2 %copy-start.10 = (bf16[2048,256]{1,0:T(8,128)(2,1)S(1)}, bf16[2048,256]{1,0:T(8,128)(2,1)}, u32[]{:S(2)}) copy-start(bf16[2048,256]{1,0:T(8,128)(2,1)} %wk.1) | copy-start | bytes 3145732
  10.9 3.2 %copy-start.2 = (bf16[1024,2048]{1,0:T(8,128)(2,1)S(1)}, bf16[1024,2048]{1,0:T(8,128)(2,1)}, u32[]{:S(2)}) copy-start(bf16[1024,2048]{1,0:T(8,128)(2,1)} %x.7) | copy-start | bytes 12582916
  27.3 1.1 copy-start.4
  28.4 1.3 %copy-start.7 = (bf16[1024,1024]{1,0:T(8,128)(2,1)}, bf16[1024,1024]{1,0:T(8,128)(2,1)S(1)}, u32[]{:S(2)}) copy-start(bf16[1024,1024]{1,0:T(8,128)(2,1)S(1)} %get-tuple-element.15.v) | copy-start | bytes 6291460
  29.7 6.9 %copy-start.11 = (bf16[160,256]{1,0:T(8,128)(2,1)}, bf16[160,256]{1,0:T(8,128)(2,1)S(1)}, u32[]{:S(2)}) copy-start(bf16[160,256]{1,0:T(8,128)(2,1)S(1)} %get-tuple-element.17) | copy-start | bytes 245764
  29.7 4.3 %collective-permute-start.1 = (bf16[160,256]{1,0:T(8,128)(2,1)S(1)}, bf16[160,256]{1,0:T(8,128)(2,1)S(1)}, u32[]{:S(2)}, u32[]{:S(2)}) collective-permute-start(bf16[160,256]{1,0:T(8,128)(2,1)S(1)} %get-tuple-element.18), channel_id=1, source_target_pairs={{0,2},{2,4},{4,6},{6,0},{1,3},{3,5},{5,7},{7,1},{8,10},{10,12},{12... | collective-permute-start | bytes 245768 | tf_op jit(solution)/shard_map/ppermute | solution.py:319
  31.0 4.6 %collective-permute-start.2 = (bf16[160,256]{1,0:T(8,128)(2,1)S(1)}, bf16[160,256]{1,0:T(8,128)(2,1)S(1)}, u32[]{:S(2)}, u32[]{:S(2)}) collective-permute-start(bf16[160,256]{1,0:T(8,128)(2,1)S(1)} %get-tuple-element.19), channel_id=1, source_target_pairs={{0,4},{2,6},{4,0},{6,2},{1,5},{3,7},{5,1},{7,3},{8,12},{10,14},{12... | collective-permute-start | bytes 245768 | tf_op jit(solution)/shard_map/ppermute | solution.py:319
  32.2 4.4 %collective-permute-start.3 = (bf16[160,256]{1,0:T(8,128)(2,1)S(1)}, bf16[160,256]{1,0:T(8,128)(2,1)S(1)}, u32[]{:S(2)}, u32[]{:S(2)}) collective-permute-start(bf16[160,256]{1,0:T(8,128)(2,1)S(1)} %get-tuple-element.20), channel_id=1, source_target_pairs={{0,6},{2,0},{4,2},{6,4},{1,7},{3,1},{5,3},{7,5},{8,14},{10,8},{12,... | collective-permute-start | bytes 245768 | tf_op jit(solution)/shard_map/ppermute | solution.py:319
  34.0 20.7 %copy-start.14 = (bf16[160,256]{1,0:T(8,128)(2,1)}, bf16[160,256]{1,0:T(8,128)(2,1)S(1)}, u32[]{:S(2)}) copy-start(bf16[160,256]{1,0:T(8,128)(2,1)S(1)} %collective-permute-done.1) | copy-start | bytes 245764
  35.5 19.2 %copy-start.16 = (bf16[160,256]{1,0:T(8,128)(2,1)}, bf16[160,256]{1,0:T(8,128)(2,1)S(1)}, u32[]{:S(2)}) copy-start(bf16[160,256]{1,0:T(8,128)(2,1)S(1)} %collective-permute-done.2) | copy-start | bytes 245764
  36.6 18.1 %copy-start.18 = (bf16[160,256]{1,0:T(8,128)(2,1)}, bf16[160,256]{1,0:T(8,128)(2,1)S(1)}, u32[]{:S(2)}) copy-start(bf16[160,256]{1,0:T(8,128)(2,1)S(1)} %collective-permute-done.3) | copy-start | bytes 245764
  37.3 38.0 %collective-permute-start.6 = (bf16[160,256]{1,0:T(8,128)(2,1)}, bf16[160,256]{1,0:T(8,128)(2,1)}, u32[]{:S(2)}, u32[]{:S(2)}) collective-permute-start(bf16[160,256]{1,0:T(8,128)(2,1)} %fusion.37), channel_id=1, source_target_pairs={{0,24},{1,25},{2,26},{3,27},{4,28},{5,29},{6,30},{7,31}} | collective-permute-start | bytes 245768 | tf_op jit(solution)/shard_map/ppermute | solution.py:315
  42.1 33.1 %collective-permute-start.5 = (bf16[160,256]{1,0:T(8,128)(2,1)}, bf16[160,256]{1,0:T(8,128)(2,1)}, u32[]{:S(2)}, u32[]{:S(2)}) collective-permute-start(bf16[160,256]{1,0:T(8,128)(2,1)} %fusion.37), channel_id=1, source_target_pairs={{0,16},{8,24},{1,17},{9,25},{2,18},{10,26},{3,19},{11,27},{4,20},{... | collective-permute-start | bytes 245768 | tf_op jit(solution)/shard_map/ppermute | solution.py:315
  44.0 31.2 %collective-permute-start.4 = (bf16[160,256]{1,0:T(8,128)(2,1)}, bf16[160,256]{1,0:T(8,128)(2,1)}, u32[]{:S(2)}, u32[]{:S(2)}) collective-permute-start(bf16[160,256]{1,0:T(8,128)(2,1)} %fusion.37), channel_id=1, source_target_pairs={{0,8},{8,16},{16,24},{1,9},{9,17},{17,25},{2,10},{10,18},{18,26},{... | collective-permute-start | bytes 245768 | tf_op jit(solution)/shard_map/ppermute | solution.py:315
  47.0 1.6 %copy-start.8 = (bf16[1024,1024]{1,0:T(8,128)(2,1)S(1)}, bf16[1024,1024]{1,0:T(8,128)(2,1)}, u32[]{:S(2)}) copy-start(bf16[1024,1024]{1,0:T(8,128)(2,1)} %copy-done.7) | copy-start | bytes 6291460
  48.6 6.1 %copy-start.3 = (bf16[1024,2048]{1,0:T(8,128)(2,1)S(1)}, bf16[1024,2048]{1,0:T(8,128)(2,1)}, u32[]{:S(2)}) copy-start(bf16[1024,2048]{1,0:T(8,128)(2,1)} %x.7) | copy-start | bytes 12582916
  54.7 4.6 %copy-start = (bf16[2048,3,1,1024]{3,0,2,1:T(8,128)(2,1)S(1)}, bf16[2048,3,1,1024]{3,0,2,1:T(8,128)(2,1)}, u32[]{:S(2)}) copy-start(bf16[2048,3,1,1024]{3,0,2,1:T(8,128)(2,1)} %param.8) | copy-start | bytes 37748740
  67.2 8.0 %copy-start.12 = (bf16[160,256]{1,0:T(8,128)(2,1)S(1)}, bf16[160,256]{1,0:T(8,128)(2,1)}, u32[]{:S(2)}) copy-start(bf16[160,256]{1,0:T(8,128)(2,1)} %copy-done.11) | copy-start | bytes 245764
  67.2 8.0 %copy-start.15 = (bf16[160,256]{1,0:T(8,128)(2,1)S(1)}, bf16[160,256]{1,0:T(8,128)(2,1)}, u32[]{:S(2)}) copy-start(bf16[160,256]{1,0:T(8,128)(2,1)} %copy-done.14) | copy-start | bytes 245764
  67.3 8.0 %copy-start.17 = (bf16[160,256]{1,0:T(8,128)(2,1)S(1)}, bf16[160,256]{1,0:T(8,128)(2,1)}, u32[]{:S(2)}) copy-start(bf16[160,256]{1,0:T(8,128)(2,1)} %copy-done.16) | copy-start | bytes 245764
  67.3 8.0 %copy-start.19 = (bf16[160,256]{1,0:T(8,128)(2,1)S(1)}, bf16[160,256]{1,0:T(8,128)(2,1)}, u32[]{:S(2)}) copy-start(bf16[160,256]{1,0:T(8,128)(2,1)} %copy-done.18) | copy-start | bytes 245764
  67.3 15.5 %copy-start.5 = (bf16[4,4,160,256]{3,2,1,0:T(8,128)(2,1)S(1)}, bf16[4,4,160,256]{3,2,1,0:T(8,128)(2,1)}, u32[]{:S(2)}) copy-start(bf16[4,4,160,256]{3,2,1,0:T(8,128)(2,1)} %copy-done.4) | copy-start | bytes 3932164
  67.3 15.5 %copy-start.6 = (bf16[256,512]{1,0:T(8,128)(2,1)S(1)}, bf16[256,512]{1,0:T(8,128)(2,1)}, u32[]{:S(2)}) copy-start(bf16[256,512]{1,0:T(8,128)(2,1)} %select_convert_fusion.first) | copy-start | bytes 786436
  67.3 15.5 %copy-start.13 = (f32[1,1024]{1,0:T(1,128)S(1)}, f32[1,1024]{1,0:T(1,128)}, u32[]{:S(2)}) copy-start(f32[1,1024]{1,0:T(1,128)} %gain.3) | copy-start | bytes 12292
  76.5 3.8 %collective-permute-start.9 = (bf16[160,256]{1,0:T(8,128)(2,1)S(1)}, bf16[160,256]{1,0:T(8,128)(2,1)S(1)}, u32[]{:S(2)}, u32[]{:S(2)}) collective-permute-start(bf16[160,256]{1,0:T(8,128)(2,1)S(1)} %get-tuple-element.21), channel_id=1, source_target_pairs={{0,6},{2,0},{4,2},{6,4},{1,7},{3,1},{5,3},{7,5},{8,14},{10,8},{12,... | collective-permute-start | bytes 245768 | tf_op jit(solution)/shard_map/ppermute | solution.py:319
  78.6 4.2 %collective-permute-start.7 = (bf16[160,256]{1,0:T(8,128)(2,1)S(1)}, bf16[160,256]{1,0:T(8,128)(2,1)S(1)}, u32[]{:S(2)}, u32[]{:S(2)}) collective-permute-start(bf16[160,256]{1,0:T(8,128)(2,1)S(1)} %get-tuple-element.22), channel_id=1, source_target_pairs={{0,2},{2,4},{4,6},{6,0},{1,3},{3,5},{5,7},{7,1},{8,10},{10,12},{12... | collective-permute-start | bytes 245768 | tf_op jit(solution)/shard_map/ppermute | solution.py:319
  78.6 4.2 %collective-permute-start.8 = (bf16[160,256]{1,0:T(8,128)(2,1)S(1)}, bf16[160,256]{1,0:T(8,128)(2,1)S(1)}, u32[]{:S(2)}, u32[]{:S(2)}) collective-permute-start(bf16[160,256]{1,0:T(8,128)(2,1)S(1)} %get-tuple-element.23), channel_id=1, source_target_pairs={{0,4},{2,6},{4,0},{6,2},{1,5},{3,7},{5,1},{7,3},{8,12},{10,14},{12... | collective-permute-start | bytes 245768 | tf_op jit(solution)/shard_map/ppermute | solution.py:319
  92.3 14.1 %collective-permute-start.10 = (bf16[512,2048]{1,0:T(8,128)(2,1)S(1)}, bf16[512,2048]{1,0:T(8,128)(2,1)S(1)}, u32[]{:S(2)}, u32[]{:S(2)}) collective-permute-start(bf16[512,2048]{1,0:T(8,128)(2,1)S(1)} %finish.3), channel_id=1, source_target_pairs={{0,1},{1,0},{2,3},{3,2},{4,5},{5,4},{6,7},{7,6},{8,9},{9,8},{10,11... | collective-permute-start | bytes 6291464 | tf_op jit(solution)/shard_map/ppermute | solution.py:356
